TPU v7x, 768 devices: a whole 4x8x12 slice. The times are simulated.
768 devices in a mesh: tile: 32 (over x, y_hi, core), kern: 24 (over z, y_lo).
Axes of the slice: x: 4, y: 8 (y_hi: 4, y_lo: 2; y = y_hi * 2 + y_lo), z: 12, core: 2. Of those that a mesh axis runs over, the one named last changes fastest.
Arguments:
- mask_pixels: bfloat16 [1152, 36864], P(None, 'tile'), may hold values from -6 to 6
- orientation: int32 [32, 2], P('tile'), may hold values 0 or 1
- target_pattern: int32 [1152, 36864], P('kern', 'tile'), may hold values 0 or 1
- kernel_real: float32 [24, 64, 64], P('kern'), may hold values from -6 to 6
- kernel_imag: float32 [24, 64, 64], P('kern'), may hold values from -6 to 6
- eigen_weights: float32 [24], P('kern'), may hold values from 0.01 to 0.1
Outputs:
- mask_gradient: float32 [1152, 36864], P('kern', 'tile')
Inputs may be any that keep to these rules, and one draw needn't show every extreme that they name: `orientation`: 1 takes the neighbour's facing strip in order, 0 reversed; the entry for a side without neighbour is unused.
All inputs are finite; a program needn't handle non-finite values. No bound on the sum of `orientation` or of `target_pattern` on one device may be relied on, other than what follows from the above.
Results may differ from a plain program's by a relative error of at most 0.018.
Values may be sent and summed in bfloat16 or wider, within the bound.
A program may use at most 64 MiB of HBM per device.

v0:
```python
import math

import jax
import jax.numpy as jnp
from jax import lax
from jax.sharding import PartitionSpec as P

N = 1152
HALO = 64
KF = 64
NE = 1280


STEEPNESS = 4.0
THRESHOLD = 1.0


def with_halo(block, sides, width):
    for axis, dim in sides:
        count = lax.axis_size(axis)
        forward = [(i, i + 1) for i in range(count - 1)]
        backward = [(target, source) for source, target in forward]
        low = lax.ppermute(
            lax.slice_in_dim(block, block.shape[dim] - width, None, axis=dim), axis, forward
        )
        high = lax.ppermute(lax.slice_in_dim(block, 0, width, axis=dim), axis, backward)
        block = jnp.concatenate([low, block, high], axis=dim)
    return block


def wave_tables(length):
    position = lax.iota(jnp.int32, length)
    frequency = lax.iota(jnp.int32, KF) - KF // 2
    phase = jnp.mod(position[:, None] * frequency[None, :], NE).astype(jnp.float32) * (
        2.0 * math.pi / NE
    )
    return (jnp.cos(phase).astype(jnp.bfloat16), jnp.sin(phase).astype(jnp.bfloat16))


def transform_tables():
    cos_full, sin_full = wave_tables(NE)
    cos_mid = cos_full[HALO : HALO + N]
    sin_mid = sin_full[HALO : HALO + N]
    full_pair = jnp.concatenate([cos_full, sin_full], 1)
    mid_pair = jnp.concatenate([cos_mid, sin_mid], 1)
    to_columns = jnp.concatenate(
        [jnp.concatenate([cos_mid.T, sin_mid.T], 1), jnp.concatenate([-sin_mid.T, cos_mid.T], 1)], 0
    )
    from_columns = jnp.concatenate(
        [jnp.concatenate([cos_mid, -sin_mid], 1), jnp.concatenate([sin_mid, cos_mid], 1)], 0
    )
    to_extended = jnp.concatenate(
        [
            jnp.concatenate([cos_full.T, sin_full.T], 1),
            jnp.concatenate([-sin_full.T, cos_full.T], 1),
        ],
        0,
    )
    return (full_pair, mid_pair, to_columns, from_columns, to_extended)


def mask_spectrum(row_spectrum, mid_pair):
    blocks = lax.dot_general(
        mid_pair, row_spectrum, (((0,), (0,)), ((), ())), preferred_element_type=jnp.float32
    )
    spec_real = blocks[:KF, :KF] - blocks[KF:, KF:]
    spec_imag = -(blocks[:KF, KF:] + blocks[KF:, :KF])
    return (spec_real, spec_imag)


def column_fields(kernel_re, kernel_im, spec_real, spec_imag, to_columns):
    scale = 1.0 / (NE * KF)
    product = (
        jnp.concatenate(
            [
                kernel_re * spec_real - kernel_im * spec_imag,
                kernel_re * spec_imag + kernel_im * spec_real,
            ],
            1,
        )
        * scale
    )
    columns = jnp.dot(
        product.astype(jnp.bfloat16), to_columns, preferred_element_type=jnp.float32
    ).astype(jnp.bfloat16)
    return jnp.concatenate([columns, jnp.concatenate([-columns[:, N:], columns[:, :N]], 1)], 0)


def intensity_term(fields, weight):
    field_real = fields[..., :N].astype(jnp.float32)
    field_imag = fields[..., N:].astype(jnp.float32)
    return weight * (field_real * field_real + field_imag * field_imag)


def resist_slope(intensity, target_rows):
    resist = jax.nn.sigmoid(STEEPNESS * (intensity - THRESHOLD))
    return (
        2.0 * (resist - target_rows.astype(jnp.float32)) * STEEPNESS * resist * (1.0 - resist)
    ).astype(jnp.bfloat16)


def weighted_fields(fields, slope):
    doubled = jnp.concatenate([slope, slope], 1).astype(jnp.float32)
    return (fields.astype(jnp.float32) * doubled).astype(jnp.bfloat16)


def adjoint_spectrum(blocks, kernel_re, kernel_im, weight):
    wave_real = blocks[:KF, :KF] + blocks[KF:, KF:]
    wave_imag = blocks[:KF, KF:] - blocks[KF:, :KF]
    factor = 2.0 * weight / (NE * KF)
    return (
        factor * (kernel_re * wave_real + kernel_im * wave_imag),
        factor * (kernel_re * wave_imag - kernel_im * wave_real),
    )


def extended_gradient(grad_real, grad_imag, row_pair, to_extended):
    combined = jnp.concatenate([grad_real, grad_imag], 1).astype(jnp.bfloat16)
    waves = jnp.dot(combined, to_extended, preferred_element_type=jnp.float32).astype(jnp.bfloat16)
    stacked = jnp.concatenate([waves[:, :NE], -waves[:, NE:]], 0)
    return jnp.dot(row_pair, stacked, preferred_element_type=jnp.float32)


def per_device(mask_pixels, orientation, target_pattern, kernel_real, kernel_imag, eigen_weights):
    full_pair, mid_pair, to_columns, from_columns, to_extended = transform_tables()
    extended = with_halo(mask_pixels, (("tile", 1),), HALO)
    left_rim = extended[:, :HALO]
    right_rim = extended[:, HALO + N :]
    left_rim = jnp.where(orientation[0, 0] == 1, left_rim, left_rim[:, ::-1])
    right_rim = jnp.where(orientation[0, 1] == 1, right_rim, right_rim[:, ::-1])
    joined = jnp.concatenate([left_rim, mask_pixels, right_rim], 1)
    row_spectrum = jnp.dot(joined, full_pair, preferred_element_type=jnp.float32)
    row_spectrum = row_spectrum.astype(jnp.bfloat16)
    spec_real, spec_imag = mask_spectrum(row_spectrum, mid_pair)
    row_count = target_pattern.shape[0]
    row_pair = lax.dynamic_slice_in_dim(mid_pair, lax.axis_index("kern") * row_count, row_count, 0)
    real_all, imag_all, weight_all = (
        lax.all_gather(kernel_real.astype(jnp.bfloat16), "kern", axis=0, tiled=True).astype(
            kernel_real.dtype
        ),
        lax.all_gather(kernel_imag.astype(jnp.bfloat16), "kern", axis=0, tiled=True).astype(
            kernel_imag.dtype
        ),
        lax.all_gather(eigen_weights.astype(jnp.bfloat16), "kern", axis=0, tiled=True).astype(
            eigen_weights.dtype
        ),
    )

    def single(one_real, one_imag):
        return column_fields(one_real, one_imag, spec_real, spec_imag, to_columns)

    stacked = jax.vmap(single)(real_all, imag_all)
    fields = jnp.einsum(
        "rj,kjx->krx", row_pair, stacked, preferred_element_type=jnp.float32
    ).astype(jnp.bfloat16)
    terms = intensity_term(fields, weight_all[:, None, None]).astype(jnp.bfloat16)
    intensity = jnp.sum(terms.astype(jnp.float32), 0)
    slope = resist_slope(intensity, target_pattern)
    weighted = weighted_fields(fields, slope)
    partial_rows = jnp.einsum(
        "krx,xj->krj", weighted, from_columns, preferred_element_type=jnp.float32
    ).astype(jnp.bfloat16)
    blocks = jnp.einsum("rj,krq->kjq", row_pair, partial_rows, preferred_element_type=jnp.float32)
    parts_real, parts_imag = jax.vmap(adjoint_spectrum)(blocks, real_all, imag_all, weight_all)
    grad_real, grad_imag = (
        lax.psum(jnp.sum(parts_real, 0).astype(jnp.bfloat16), "kern").astype(jnp.float32),
        lax.psum(jnp.sum(parts_imag, 0).astype(jnp.bfloat16), "kern").astype(jnp.float32),
    )
    gradient_ext = extended_gradient(grad_real, grad_imag, row_pair, to_extended)
    left_send = gradient_ext[:, :HALO]
    right_send = gradient_ext[:, HALO + N :]
    left_send = jnp.where(orientation[0, 0] == 1, left_send, left_send[:, ::-1])
    right_send = jnp.where(orientation[0, 1] == 1, right_send, right_send[:, ::-1])
    returned = with_halo(jnp.concatenate([left_send, right_send], 1), (("tile", 1),), HALO)
    middle = jnp.zeros((row_count, N - 2 * HALO), jnp.float32)
    return gradient_ext[:, HALO : HALO + N] + jnp.concatenate(
        [returned[:, :HALO], middle, returned[:, 3 * HALO :]], 1
    )


def solution(mesh):
    in_specs = (
        P(None, "tile"),
        P("tile", None),
        P("kern", "tile"),
        P("kern", None, None),
        P("kern", None, None),
        P("kern"),
    )
    out_specs = P("kern", "tile")
    return jax.shard_map(
        per_device, mesh=mesh, in_specs=in_specs, out_specs=out_specs, check_vma=False
    )
```

profile of v0, /device:TPU:1, one launch (start us, length us, event | category | flops | bytes accessed | tf_op | source)
XLA Modules:
  0.0 321.4 jit_solution(15731256408242802016)
XLA Ops:
  0.0 2.1 fusion.93
  2.1 12.4 %collective-permute-start.1 = (bf16[1152,64]{1,0:T(8,128)(2,1)}, bf16[1152,64]{1,0:T(8,128)(2,1)}, u32[]{:S(2)}, u32[]{:S(2)}) collective-permute-start(bf16[1152,64]{1,0:T(8,128)(2,1)} %get-tuple-element.11), channel_id=1, source_target_pairs={{24,0},{48,24},{72,48},{96,72},{120,96},{144,120},{168,144},{192,1... | collective-permute-start | bytes 442376 | tf_op jit(solution)/shard_map/ppermute | solution.py:26
  14.5 1.9 collective-permute-start
  16.5 1.5 sine_convert_fusion.1
  18.0 0.0 copy-start.1
  18.0 0.0 copy-start.2
  18.0 0.9 slice_negate_fusion.2
  19.6 1.3 dynamic-slice
  20.9 0.8 dynamic-update-slice
  21.6 0.8 bitcast_negate_fusion
  22.4 41.8 %all-reduce = bf16[24]{0:T(256)(128)(2,1)S(1)} all-reduce(bf16[24]{0:T(256)(128)(2,1)S(1)} %dynamic-update-slice), channel_id=1, replica_groups=mesh['tile'=32,'kern'=24] {'kern'}, use_global_device_ids=true, to_apply=%add | all-reduce | flops 24 | bytes 96
  64.2 2.2 sine_convert_fusion
  66.3 2.0 fusion.72
  68.3 1.4 fusion.97
  71.0 0.8 fusion.96
  71.8 0.8 convert_element_type.147
  72.6 0.8 convert_element_type.150
  73.4 0.0 copy-done.1
  73.4 0.0 copy-done.2
  73.4 35.9 %all_gather.10 = bf16[24,64,64]{2,1,0:T(8,128)(2,1)S(1)} all-gather(bf16[1,64,64]{2,1,0:T(8,128)(2,1)S(1)} %convert_element_type.147), channel_id=1, replica_groups=mesh['tile'=32,'kern'=24] {'kern'}, dimensions={0}, use_global_device_ids=true | all-gather | bytes 204800 | tf_op jit(solution)/shard_map/all_gather | solution.py:138
  109.3 37.8 %all_gather.11 = bf16[24,64,64]{2,1,0:T(8,128)(2,1)S(1)} all-gather(bf16[1,64,64]{2,1,0:T(8,128)(2,1)S(1)} %convert_element_type.150), channel_id=1, replica_groups=mesh['tile'=32,'kern'=24] {'kern'}, dimensions={0}, use_global_device_ids=true | all-gather | bytes 204800 | tf_op jit(solution)/shard_map/all_gather | solution.py:141
  147.0 0.0 collective-permute-done.1
  147.0 5.2 %rev.13 = bf16[1152,64]{1,0:T(8,128)(2,1)} reverse(bf16[1152,64]{1,0:T(8,128)(2,1)} %collective-permute-done.1), dimensions={1} | reverse | bytes 294912 | tf_op jit(solution)/shard_map/rev | solution.py:130
  152.2 0.0 collective-permute-done
  152.2 5.2 %rev.12 = bf16[1152,64]{1,0:T(8,128)(2,1)} reverse(bf16[1152,64]{1,0:T(8,128)(2,1)} %collective-permute-done), dimensions={1} | reverse | bytes 294912 | tf_op jit(solution)/shard_map/rev | solution.py:129
  157.4 1.7 broadcast_select_fusion
  159.1 1.7 broadcast_select_fusion.1
  160.8 0.0 copy-done
  160.8 5.5 %concatenate.63 = bf16[1152,1280]{1,0:T(8,128)(2,1)} concatenate(bf16[1152,64]{1,0:T(8,128)(2,1)} %broadcast_select_fusion.1, bf16[1152,1152]{1,0:T(8,128)(2,1)S(1)} %copy-done, bf16[1152,64]{1,0:T(8,128)(2,1)} %broadcast_select_fusion), dimensions={1} | concatenate | bytes 5898240 | tf_op jit(solution)/shard_map/concatenate | solution.py:131
  166.3 3.2 fusion.15
  169.5 0.1 slice_subtract_fusion.1
  169.6 0.2 fusion.16
  169.8 0.0 copy-done.5
  169.8 0.0 copy-done.6
  169.8 0.0 copy-done.7
  169.8 2.1 convolution_convert_fusion
  171.9 0.0 copy-start.3
  171.9 0.0 copy-start.4
  171.9 3.4 %slice_negate_fusion = (bf16[24,64,1152]{2,1,0:T(8,128)(2,1)}, bf16[24,64,1152]{2,1,0:T(8,128)(2,1)}) fusion(bf16[24,64,2304]{2,1,0:T(8,128)(2,1)S(1)} %convolution_convert_fusion), kind=kLoop, calls=%fused_computation.14 | loop fusion | flops 1769472 | bytes 14155776 | tf_op jit(solution)/shard_map/vmap()/neg | solution.py:86
  175.4 0.0 copy-done.3
  175.4 0.0 copy-done.4
  175.4 6.1 %fusion.11 = bf16[24,48,2304]{2,1,0:T(8,128)(2,1)} fusion(bf16[24,64,1152]{2,1,0:T(8,128)(2,1)} %get-tuple-element.10, bf16[24,64,1152]{2,1,0:T(8,128)(2,1)} %get-tuple-element.9, bf16[24,64,2304]{2,1,0:T(8,128)(2,1)S(1)} %convolution_convert_fusion, s32[]{:T(128)S(6)} %select_n.67, bf16[1152,64]{0,1:T(8,128)(2,1)S(1)} %copy-done.3, ...), kind=kOutput, calls=%fused_computation.13 | convolution fusion | flops 724623360 | bytes 19759108 | tf_op jit(solution)/shard_map/rj,kjx->krx/dot_general | solution.py:153
  181.5 3.8 %convert_reduce_fusion = f32[48,1152]{1,0:T(8,128)S(1)} fusion(bf16[24,48,2304]{2,1,0:T(8,128)(2,1)} %fusion.11, f32[24]{0:T(128)S(1)} %convert_element_type.146), kind=kLoop, calls=%fused_computation.11 | loop fusion | flops 11888640 | bytes 5529696 | tf_op jit(solution)/shard_map/reduce_sum | solution.py:157
  185.3 0.0 copy-done.8
  185.3 0.1 multiply_convert_fusion.7
  185.5 4.5 %convolution_bitcast_fusion = f32[24,128,128]{2,1,0:T(8,128)S(1)} fusion(bf16[24,48,2304]{2,1,0:T(8,128)(2,1)} %fusion.11, f32[48,2304]{1,0:T(8,128)S(1)} %maximum_convert_fusion, bf16[1152,64]{0,1:T(8,128)(2,1)S(1)} %copy-done.3, bf16[1152,64]{0,1:T(8,128)(2,1)S(1)} %copy-done.4, bf16[1152,64]{0,1:T(8,128)(2,1)} %get-tuple-element.21, s32[]{:T(128)S(6)} %select_n.67), kind=kOutput, calls=%fused_computation.17 | convolution fusion | flops 727719936 | bytes 8060932 | tf_op jit(solution)/shard_map/rj,krq->kjq/dot_general | solution.py:163
  190.0 0.0 copy-start.9
  190.0 0.0 copy-start.10
  190.0 0.0 copy-start.11
  190.0 0.6 fusion.20
  190.6 68.3 %all-reduce.1 = (bf16[64,64]{1,0:T(8,128)(2,1)S(1)}, bf16[64,64]{1,0:T(8,128)(2,1)S(1)}) all-reduce(bf16[64,64]{1,0:T(8,128)(2,1)S(1)} %get-tuple-element.6, bf16[64,64]{1,0:T(8,128)(2,1)S(1)} %get-tuple-element.5), channel_id=1, replica_groups=mesh['tile'=32,'kern'=24] {'kern'}, use_global_device_ids=true, to_apply=%region_4.5 | all-reduce | flops 8192 | bytes 32768 | tf_op jit(solution)/shard_map/psum | solution.py:167
  258.9 0.0 copy-done.11
  258.9 0.3 convolution_convert_fusion.1
  259.3 0.3 fusion.62
  259.6 0.1 fusion.95
  259.7 0.1 rev.14
  259.8 0.1 rev.15
  259.9 0.1 broadcast_select_fusion.2
  259.9 54.4 %collective-permute-start.2 = (f32[48,64]{1,0:T(8,128)S(1)}, f32[48,64]{1,0:T(8,128)S(1)}, u32[]{:S(2)}, u32[]{:S(2)}) collective-permute-start(f32[48,64]{1,0:T(8,128)S(1)} %get-tuple-element.18), channel_id=1, source_target_pairs={{0,24},{24,48},{48,72},{72,96},{96,120},{120,144},{144,168},{168,1... | collective-permute-start | bytes 36872 | tf_op jit(solution)/shard_map/ppermute | solution.py:23
  314.3 1.9 collective-permute-start.3
  316.3 0.0 collective-permute-done.2
  316.3 4.1 %collective-permute-done.3 = f32[48,64]{1,0:T(8,128)S(1)} collective-permute-done((f32[48,64]{1,0:T(8,128)S(1)}, f32[48,64]{1,0:T(8,128)S(1)}, u32[]{:S(2)}, u32[]{:S(2)}) %collective-permute-start.3) | collective-permute-done | bytes 12320 | tf_op jit(solution)/shard_map/ppermute | solution.py:26
  320.4 0.2 concatenate.80
  320.6 0.8 slice_add_fusion.1
  (14 shorter events, 0.1 us)
Async XLA Ops:
  0.0 160.8 %copy-start = (bf16[1152,1152]{1,0:T(8,128)(2,1)S(1)}, bf16[1152,1152]{1,0:T(8,128)(2,1)}, u32[]{:S(2)}) copy-start(bf16[1152,1152]{1,0:T(8,128)(2,1)} %param.6) | copy-start | bytes 7962628
  2.1 144.9 %collective-permute-start.1 = (bf16[1152,64]{1,0:T(8,128)(2,1)}, bf16[1152,64]{1,0:T(8,128)(2,1)}, u32[]{:S(2)}, u32[]{:S(2)}) collective-permute-start(bf16[1152,64]{1,0:T(8,128)(2,1)} %get-tuple-element.11), channel_id=1, source_target_pairs={{24,0},{48,24},{72,48},{96,72},{120,96},{144,120},{168,144},{192,1... | collective-permute-start | bytes 442376 | tf_op jit(solution)/shard_map/ppermute | solution.py:26
  14.5 137.7 %collective-permute-start = (bf16[1152,64]{1,0:T(8,128)(2,1)}, bf16[1152,64]{1,0:T(8,128)(2,1)}, u32[]{:S(2)}, u32[]{:S(2)}) collective-permute-start(bf16[1152,64]{1,0:T(8,128)(2,1)} %get-tuple-element.12), channel_id=1, source_target_pairs={{0,24},{24,48},{48,72},{72,96},{96,120},{120,144},{144,168},{168,1... | collective-permute-start | bytes 442376 | tf_op jit(solution)/shard_map/ppermute | solution.py:23
  18.0 55.3 %copy-start.1 = (bf16[1280,64]{0,1:T(8,128)(2,1)}, bf16[1280,64]{0,1:T(8,128)(2,1)S(1)}, u32[]{:S(2)}) copy-start(bf16[1280,64]{0,1:T(8,128)(2,1)S(1)} %get-tuple-element.30) | copy-start | bytes 491524
  18.0 55.3 %copy-start.2 = (bf16[1280,64]{0,1:T(8,128)(2,1)}, bf16[1280,64]{0,1:T(8,128)(2,1)S(1)}, u32[]{:S(2)}) copy-start(bf16[1280,64]{0,1:T(8,128)(2,1)S(1)} %get-tuple-element.31) | copy-start | bytes 491524
  166.3 3.5 %copy-start.5 = (bf16[64,1152]{1,0:T(8,128)(2,1)S(1)}, bf16[64,1152]{1,0:T(8,128)(2,1)}, u32[]{:S(2)}) copy-start(bf16[64,1152]{1,0:T(8,128)(2,1)} %get-tuple-element.25) | copy-start | bytes 442372
  166.3 3.6 %copy-start.6 = (bf16[64,1152]{1,0:T(8,128)(2,1)S(1)}, bf16[64,1152]{1,0:T(8,128)(2,1)}, u32[]{:S(2)}) copy-start(bf16[64,1152]{1,0:T(8,128)(2,1)} %bitcast_negate_fusion) | copy-start | bytes 442372
  166.3 3.6 %copy-start.7 = (bf16[64,1152]{1,0:T(8,128)(2,1)S(1)}, bf16[64,1152]{1,0:T(8,128)(2,1)}, u32[]{:S(2)}) copy-start(bf16[64,1152]{1,0:T(8,128)(2,1)} %get-tuple-element.22) | copy-start | bytes 442372
  171.9 3.4 %copy-start.3 = (bf16[1152,64]{0,1:T(8,128)(2,1)S(1)}, bf16[1152,64]{0,1:T(8,128)(2,1)}, u32[]{:S(2)}) copy-start(bf16[1152,64]{0,1:T(8,128)(2,1)} %get-tuple-element.24) | copy-start | bytes 442372
  171.9 3.4 %copy-start.4 = (bf16[1152,64]{0,1:T(8,128)(2,1)S(1)}, bf16[1152,64]{0,1:T(8,128)(2,1)}, u32[]{:S(2)}) copy-start(bf16[1152,64]{0,1:T(8,128)(2,1)} %get-tuple-element.23) | copy-start | bytes 442372
  181.5 3.8 %copy-start.8 = (s32[48,1152]{1,0:T(8,128)S(1)}, s32[48,1152]{1,0:T(8,128)}, u32[]{:S(2)}) copy-start(s32[48,1152]{1,0:T(8,128)} %param.8) | copy-start | bytes 663556
  190.0 68.9 %copy-start.9 = (bf16[64,1280]{1,0:T(8,128)(2,1)S(1)}, bf16[64,1280]{1,0:T(8,128)(2,1)}, u32[]{:S(2)}) copy-start(bf16[64,1280]{1,0:T(8,128)(2,1)} %get-tuple-element.32) | copy-start | bytes 491524
  190.0 68.9 %copy-start.10 = (bf16[64,1280]{1,0:T(8,128)(2,1)S(1)}, bf16[64,1280]{1,0:T(8,128)(2,1)}, u32[]{:S(2)}) copy-start(bf16[64,1280]{1,0:T(8,128)(2,1)} %get-tuple-element.33) | copy-start | bytes 491524
  190.0 68.9 %copy-start.11 = (bf16[64,1280]{1,0:T(8,128)(2,1)S(1)}, bf16[64,1280]{1,0:T(8,128)(2,1)}, u32[]{:S(2)}) copy-start(bf16[64,1280]{1,0:T(8,128)(2,1)} %fusion.72) | copy-start | bytes 491524
  259.9 56.3 %collective-permute-start.2 = (f32[48,64]{1,0:T(8,128)S(1)}, f32[48,64]{1,0:T(8,128)S(1)}, u32[]{:S(2)}, u32[]{:S(2)}) collective-permute-start(f32[48,64]{1,0:T(8,128)S(1)} %get-tuple-element.18), channel_id=1, source_target_pairs={{0,24},{24,48},{48,72},{72,96},{96,120},{120,144},{144,168},{168,1... | collective-permute-start | bytes 36872 | tf_op jit(solution)/shard_map/ppermute | solution.py:23
  314.3 6.0 %collective-permute-start.3 = (f32[48,64]{1,0:T(8,128)S(1)}, f32[48,64]{1,0:T(8,128)S(1)}, u32[]{:S(2)}, u32[]{:S(2)}) collective-permute-start(f32[48,64]{1,0:T(8,128)S(1)} %get-tuple-element.17), channel_id=1, source_target_pairs={{24,0},{48,24},{72,48},{96,72},{120,96},{144,120},{168,144},{192,1... | collective-permute-start | bytes 36872 | tf_op jit(solution)/shard_map/ppermute | solution.py:26
where the time goes:
time: 325 us; the launch traced here: 321 us
  blocking collectives  184 us (57%)
  starting transfers between devices  70.7 us (22%)
  local copies, waits for them, and re-layouts  22.6 us (7%)
  other arithmetic  21.5 us (7%)
  matrix products  16.6 us (5%)
  waiting for transfers between devices  4.11 us (1%)
    psum x1, blocking collectives, per_device(): lax.psum(jnp.sum(parts_imag, 0).astype(jnp.bfloat16), 'kern')  68.3 us
    ppermute x2, starting transfers between devices, with_halo(): lax.ppermute(lax.slice_in_dim(block, block.shape[dim] - width, None, axis...  56.3 us
    unnamed x1, blocking collectives  41.8 us
    all_gather x1, blocking collectives, per_device(): lax.all_gather(kernel_imag.astype(jnp.bfloat16), 'kern', axis=0, tiled=True)  37.8 us
    all_gather x1, blocking collectives, per_device(): lax.all_gather(kernel_real.astype(jnp.bfloat16), 'kern', axis=0, tiled=True)  35.9 us
    ppermute x2, starting transfers between devices, with_halo(): lax.ppermute(lax.slice_in_dim(block, 0, width, axis=dim), axis, backward)  14.3 us
  transfers between devices with their start and end apart: 4, of which 1 were waited for; matrix products, arithmetic and copies ran while one was open for 6% of the time, Pallas kernels for 0%

commit v1 on v0

v1 whole, which is shorter than its diff:
```python
import math

import jax
import jax.numpy as jnp
import ml_dtypes
import numpy as np
from jax import lax
from jax.experimental import pallas as pl
from jax.experimental.pallas import tpu as pltpu
from jax.sharding import PartitionSpec as P

N = 1152
HALO = 64
KF = 64
NE = 1280
LANES = 128
CHUNKS = N // LANES
GROUP = 4

STEEPNESS = 4.0
THRESHOLD = 1.0
F32 = jnp.float32
BF16 = jnp.bfloat16
MESH = pl.DeviceIdType.MESH


def wave_pair():
    phase = np.mod(np.arange(NE)[:, None] * (np.arange(KF) - KF // 2)[None, :], NE).astype(np.float32)
    phase = phase * np.float32(2.0 * math.pi / NE)
    return np.concatenate([np.cos(phase), np.sin(phase)], 1).astype(ml_dtypes.bfloat16)


def tables(ranks):
    full = wave_pair()
    mid = full[HALO : HALO + N]
    right, left = full[HALO + N :], full[:HALO]
    rim = np.stack([np.concatenate([right, left]), np.concatenate([right[::-1], left[::-1]])])
    rows_t = np.transpose(mid.reshape(ranks, N // ranks, 2 * KF), (0, 2, 1))
    return mid, mid.T.copy(), rows_t.copy(), rim, np.transpose(rim, (0, 2, 1)).copy()


def dot(a, b):
    return jnp.dot(a, b, preferred_element_type=F32)


def body(
    ranks,
    orient,
    weight,
    mask_hbm,
    target_hbm,
    hr_hbm,
    hi_hbm,
    mid_hbm,
    mid_t_hbm,
    rows_t_hbm,
    rim_ref,
    rim_t_ref,
    out_ref,
    mask,
    target,
    hr,
    hi,
    mid,
    mid_t,
    rows,
    rows_t,
    spec_all,
    part_all,
    strip,
    halo_low,
    halo_high,
    columns,
    stacked,
    lines,
    to_cols,
    from_cols,
    fields,
    partial,
    margin,
    margin_low,
    margin_high,
    local_sem,
    spec_send,
    spec_recv,
    part_send,
    part_recv,
    tile_send,
    tile_recv,
):
    tiles = lax.axis_size("tile")
    tile = lax.axis_index("tile")
    rank = lax.axis_index("kern")
    up = lax.rem(tile + 1, tiles)
    down = lax.rem(tile + tiles - 1, tiles)
    count = N // ranks

    def load(src, dst, slot):
        copy = pltpu.make_async_copy(src, dst, local_sem.at[slot])
        copy.start()
        return copy

    barrier = pltpu.get_barrier_semaphore()
    for step in range(1, ranks):
        pl.semaphore_signal(
            barrier, inc=1, device_id={"kern": lax.rem(rank + step, ranks)}, device_id_type=MESH
        )
    for other in (up, down):
        pl.semaphore_signal(barrier, inc=1, device_id={"tile": other}, device_id_type=MESH)

    get_hr = load(hr_hbm.at[0], hr, 0)
    get_hi = load(hi_hbm.at[0], hi, 1)
    get_mid_t = load(mid_t_hbm, mid_t, 2)
    get_first = load(mask_hbm.at[:, 0:LANES], mask.at[:, 0:LANES], 3)
    get_last = load(mask_hbm.at[:, N - LANES : N], mask.at[:, N - LANES : N], 4)
    get_inner = load(mask_hbm.at[:, LANES : N - LANES], mask.at[:, LANES : N - LANES], 5)
    get_mid = load(mid_hbm, mid, 6)
    get_rows = load(mid_hbm.at[pl.ds(pl.multiple_of(rank * count, 16), count)], rows, 7)
    get_rows_t = load(rows_t_hbm.at[rank], rows_t, 8)
    get_target = load(target_hbm, target, 9)

    low = lax.broadcasted_iota(jnp.int32, (KF, 2 * KF), 1) < KF
    plus = jnp.where(low, 1.0, -1.0)
    minus = -plus

    def swap(x):
        return pltpu.roll(x, KF, 1)

    get_hr.wait()
    get_hi.wait()
    root = jnp.sqrt(jnp.full((KF, 2 * KF), weight[0], F32))
    spec_all[rank] = (jnp.concatenate([hr[...], hi[...]], 1) * root).astype(BF16)

    pl.semaphore_wait(barrier, ranks + 1)

    spec_copies = []
    for step in range(1, ranks):
        copy = pltpu.make_async_remote_copy(
            src_ref=spec_all.at[rank],
            dst_ref=spec_all.at[rank],
            send_sem=spec_send.at[step],
            recv_sem=spec_recv.at[step],
            device_id={"kern": lax.rem(rank + step, ranks)},
            device_id_type=MESH,
        )
        copy.start()
        spec_copies.append(copy)

    def to_neighbours(src, dst_up, dst_down, first):
        copies = []
        for place, (dst, other) in enumerate(((dst_up, up), (dst_down, down))):
            copy = pltpu.make_async_remote_copy(
                src_ref=src,
                dst_ref=dst,
                send_sem=tile_send.at[first + place],
                recv_sem=tile_recv.at[first + place],
                device_id={"tile": other},
                device_id_type=MESH,
            )
            copy.start()
            copies.append(copy)
        return copies

    get_mid_t.wait()
    get_first.wait()
    get_last.wait()
    first = dot(mid_t[...], mask[:, 0:LANES]).astype(BF16)
    last = dot(mid_t[...], mask[:, N - LANES : N]).astype(BF16)
    columns[:, 0:LANES] = first
    columns[:, N - LANES : N] = last
    edge = lax.broadcasted_iota(jnp.int32, (2 * KF, LANES), 1) < HALO
    strip[...] = jnp.where(edge, first.astype(F32), last.astype(F32)).astype(BF16)
    halo_copies = to_neighbours(strip, halo_low, halo_high, 0)

    get_inner.wait()
    for j in range(1, CHUNKS - 1):
        columns[:, j * LANES : (j + 1) * LANES] = dot(
            mid_t[...], mask[:, j * LANES : (j + 1) * LANES]
        ).astype(BF16)

    get_mid.wait()
    wide = lax.broadcasted_iota(jnp.int32, (LANES, 2 * KF), 1) < KF
    for j in range(CHUNKS):
        part = mid_t[:, j * LANES : (j + 1) * LANES]
        to_cols[j, 0:KF, 0:LANES] = part[:KF]
        to_cols[j, 0:KF, LANES:] = part[KF:]
        to_cols[j, KF:, 0:LANES] = -part[KF:]
        to_cols[j, KF:, LANES:] = part[:KF]
        block = mid[j * LANES : (j + 1) * LANES].astype(F32)
        from_cols[j, 0:LANES] = jnp.where(wide, block, -block).astype(BF16)
        from_cols[j, LANES:] = swap(block).astype(BF16)

    keep_right = orient[0, 1].astype(F32)
    keep_left = orient[0, 0].astype(F32)

    blocks = dot(columns[...], mid[...])
    upper = lax.broadcasted_iota(jnp.int32, (LANES, LANES), 0) < HALO
    keep = jnp.where(upper, keep_right, keep_left)
    rim = keep * rim_ref[0].astype(F32) + (1.0 - keep) * rim_ref[1].astype(F32)
    there = jnp.where(upper, jnp.where(tile < tiles - 1, 1.0, 0.0), jnp.where(tile > 0, 1.0, 0.0))
    rim = (rim * there).astype(BF16)
    for copy in halo_copies:
        copy.wait_recv()
    halo = jnp.where(edge, halo_high[...].astype(F32), halo_low[...].astype(F32)).astype(BF16)
    blocks = blocks + dot(halo, rim)
    lower = swap(blocks[KF:])
    spec = jnp.where(low, blocks[:KF] - lower, -(blocks[:KF] + lower)) * (1.0 / (NE * KF))
    spec_turned = swap(spec) * minus

    def kernel_parts(k):
        both = spec_all[k].astype(F32)
        other = swap(both)
        return jnp.where(low, both, other), jnp.where(low, other, both)

    get_rows.wait()
    for copy in spec_copies:
        copy.wait_recv()
    for k in range(ranks):
        real, imag = kernel_parts(k)
        product = real * spec + imag * spec_turned
        stacked[0:KF, k * LANES : (k + 1) * LANES] = product.astype(BF16)
        stacked[KF:, k * LANES : (k + 1) * LANES] = (swap(product) * minus).astype(BF16)
    for k in range(0, ranks, 2):
        pair = dot(rows[...], stacked[:, k * LANES : (k + 2) * LANES]).astype(BF16)
        lines[k * count : (k + 1) * count] = pair[:, :LANES]
        lines[(k + 1) * count : (k + 2) * count] = pair[:, LANES:]
    partial[...] = jnp.zeros_like(partial)
    get_target.wait()

    size = GROUP * count

    def chunk(j, carry):
        total = jnp.zeros((count, LANES), F32)
        for b in range(ranks // GROUP):
            field = dot(lines[b * size : (b + 1) * size], to_cols[j])
            for i in range(GROUP):
                one = field[i * count : (i + 1) * count]
                total = total + (one[:, :LANES] * one[:, :LANES] + one[:, LANES:] * one[:, LANES:])
            fields[b * size : (b + 1) * size] = field.astype(BF16)
        wanted = target[:, pl.ds(pl.multiple_of(j * LANES, LANES), LANES)].astype(F32)
        resist = 1.0 / (1.0 + jnp.exp(-STEEPNESS * (total - THRESHOLD)))
        slope = (2.0 * (resist - wanted) * STEEPNESS * resist * (1.0 - resist)).astype(BF16)
        slope = jnp.concatenate([slope, slope], 1)
        slope = jnp.concatenate([slope] * GROUP, 0)
        for b in range(ranks // GROUP):
            weighted = fields[b * size : (b + 1) * size] * slope
            partial[b * size : (b + 1) * size] += dot(weighted, from_cols[j])
        return carry

    lax.fori_loop(0, CHUNKS, chunk, 0)

    get_rows_t.wait()
    grad = jnp.zeros((KF, 2 * KF), F32)
    for k in range(0, ranks, 2):
        pair = jnp.concatenate(
            [
                partial[k * count : (k + 1) * count].astype(BF16),
                partial[(k + 1) * count : (k + 2) * count].astype(BF16),
            ],
            1,
        )
        wave = dot(rows_t[...], pair)
        for i in range(2):
            one = wave[:, i * LANES : (i + 1) * LANES]
            one = one[:KF] + swap(one[KF:]) * plus
            real, imag = kernel_parts(k + i)
            grad = grad + real * one + imag * (swap(one) * plus)
    part_all[rank] = (grad * (2.0 / (NE * KF))).astype(BF16)

    part_copies = []
    for step in range(1, ranks):
        copy = pltpu.make_async_remote_copy(
            src_ref=part_all.at[rank],
            dst_ref=part_all.at[rank],
            send_sem=part_send.at[step],
            recv_sem=part_recv.at[step],
            device_id={"kern": lax.rem(rank + step, ranks)},
            device_id_type=MESH,
        )
        copy.start()
        part_copies.append(copy)
    for copy in part_copies:
        copy.wait_recv()
    grad = jnp.zeros((KF, 2 * KF), F32)
    for k in range(ranks):
        grad = grad + part_all[k].astype(F32)
    grad = grad.astype(BF16).astype(F32)
    both = jnp.concatenate([grad, swap(grad) * minus], 0).astype(BF16)
    line = dot(rows[...], both)
    side = lax.broadcasted_iota(jnp.int32, (count, 2 * KF), 1) < KF
    line = jnp.where(side, line, -line).astype(BF16)
    first_lanes = lax.broadcasted_iota(jnp.int32, (LANES, LANES), 1) < HALO
    keep = jnp.where(first_lanes, keep_right, keep_left)
    rim = keep * rim_t_ref[0].astype(F32) + (1.0 - keep) * rim_t_ref[1].astype(F32)
    margin[...] = dot(line, rim.astype(BF16))
    margin_copies = to_neighbours(margin, margin_low, margin_high, 2)
    out_ref[...] = dot(line, mid_t[...])
    for copy in margin_copies:
        copy.wait_recv()
    out_ref[:, 0:LANES] += jnp.where(jnp.logical_and(side, tile > 0), margin_low[...], 0.0)
    out_ref[:, N - LANES : N] += jnp.where(
        jnp.logical_and(jnp.logical_not(side), tile < tiles - 1), margin_high[...], 0.0
    )
    for copy in spec_copies + halo_copies + part_copies + margin_copies:
        copy.wait_send()


def solution(mesh):
    ranks = mesh.shape["kern"]
    count = N // ranks
    mid, mid_t, rows_t, rim, rim_t = tables(ranks)

    def per_device(mask, orientation, target, kernel_real, kernel_imag, eigen_weights):
        hbm = pl.BlockSpec(memory_space=pl.ANY)
        vmem = pl.BlockSpec(memory_space=pltpu.VMEM)
        smem = pl.BlockSpec(memory_space=pltpu.SMEM)
        return pl.pallas_call(
            lambda *refs: body(ranks, *refs),
            out_shape=jax.ShapeDtypeStruct((count, N), F32),
            in_specs=[smem, smem] + [hbm] * 7 + [vmem] * 2,
            out_specs=vmem,
            scratch_shapes=[
                pltpu.VMEM((N, N), BF16),
                pltpu.VMEM((count, N), jnp.int32),
                pltpu.VMEM((KF, KF), F32),
                pltpu.VMEM((KF, KF), F32),
                pltpu.VMEM((N, LANES), BF16),
                pltpu.VMEM((LANES, N), BF16),
                pltpu.VMEM((count, LANES), BF16),
                pltpu.VMEM((LANES, count), BF16),
                pltpu.VMEM((ranks, KF, LANES), BF16),
                pltpu.VMEM((ranks, KF, LANES), BF16),
                pltpu.VMEM((LANES, LANES), BF16),
                pltpu.VMEM((LANES, LANES), BF16),
                pltpu.VMEM((LANES, LANES), BF16),
                pltpu.VMEM((LANES, N), BF16),
                pltpu.VMEM((LANES, ranks * LANES), BF16),
                pltpu.VMEM((N, LANES), BF16),
                pltpu.VMEM((CHUNKS, LANES, 2 * LANES), BF16),
                pltpu.VMEM((CHUNKS, 2 * LANES, LANES), BF16),
                pltpu.VMEM((N, 2 * LANES), BF16),
                pltpu.VMEM((N, LANES), F32),
                pltpu.VMEM((count, LANES), F32),
                pltpu.VMEM((count, LANES), F32),
                pltpu.VMEM((count, LANES), F32),
                pltpu.SemaphoreType.DMA((10,)),
                pltpu.SemaphoreType.DMA((ranks,)),
                pltpu.SemaphoreType.DMA((ranks,)),
                pltpu.SemaphoreType.DMA((ranks,)),
                pltpu.SemaphoreType.DMA((ranks,)),
                pltpu.SemaphoreType.DMA((4,)),
                pltpu.SemaphoreType.DMA((4,)),
            ],
            compiler_params=pltpu.CompilerParams(collective_id=0, has_side_effects=True),
        )(
            orientation,
            eigen_weights,
            mask,
            target,
            kernel_real,
            kernel_imag,
            jnp.asarray(mid),
            jnp.asarray(mid_t),
            jnp.asarray(rows_t),
            jnp.asarray(rim),
            jnp.asarray(rim_t),
        )

    in_specs = (
        P(None, "tile"),
        P("tile", None),
        P("kern", "tile"),
        P("kern", None, None),
        P("kern", None, None),
        P("kern"),
    )
    return jax.shard_map(
        per_device, mesh=mesh, in_specs=in_specs, out_specs=P("kern", "tile"), check_vma=False
    )
```

time: 325 us -> 65.6 us (0.20)
  the two profiles are of different devices: /device:TPU:1 before, /device:TPU:17 now
where the time goes in v1:
time: 65.6 us; the launch traced here: 65.4 us
  Pallas kernels  63.1 us (96%)
  local copies, waits for them, and re-layouts  1.64 us (2%)
  between operations  0.66 us (1%)
    pallas_call x1, Pallas kernels, per_device(): pl.pallas_call(lambda *refs: body(ranks, *refs), out_shape=jax.ShapeDtype...  63.1 us
    unnamed x1, local copies, waits for them, and re-layouts  1.64 us

profile of v1, /device:TPU:17, one launch (start us, length us, event | category | flops | bytes accessed | tf_op | source)
XLA Modules:
  0.0 65.4 jit_solution(10080050080959218132)
XLA Ops:
  0.7 63.1 %shard_map.109 = f32[48,1152]{1,0:T(8,128)} custom-call(s32[1,2]{1,0:T(1,128)} %refs_0_.1, f32[1]{0:T(128)S(6)} %copy.13.refs_1_, bf16[1152,1152]{1,0:T(8,128)(2,1)} %refs_2_.1, s32[48,1152]{1,0:T(8,128)} %refs_3_.1, f32[1,64,64]{2,1,0:T(8,128)} %refs_4_.1, f32[1,64,64]{2,1,0:T(8,128)} %refs_5_.1, bf16[1152,128]{1,0:T(8,128)(2,1)} %constant.10.clone.refs_6_, ...), custom_call_target="tpu_custom_call" | custom-call | tf_op jit(solution)/shard_map/pallas_call | solution.py:317
  63.7 1.6 %copy.14 = f32[48,1152]{1,0:T(8,128)} copy(f32[48,1152]{1,0:T(8,128)} %shard_map.109) | data formatting | bytes 442368

commit v2 on v1

--- a/solution.py
+++ b/solution.py
@@ -15,7 +15,9 @@
 NE = 1280
 LANES = 128
 CHUNKS = N // LANES
-GROUP = 4
+GROUP = 2
+BATCH = 4
+HUBS = 2
 
 STEEPNESS = 4.0
 THRESHOLD = 1.0
@@ -72,7 +74,8 @@
     halo_high,
     columns,
     stacked,
-    lines,
+    intensity,
+    whole,
     to_cols,
     from_cols,
     fields,
@@ -85,6 +88,8 @@
     spec_recv,
     part_send,
     part_recv,
+    sum_send,
+    sum_recv,
     tile_send,
     tile_recv,
 ):
@@ -101,10 +106,12 @@
         return copy
 
     barrier = pltpu.get_barrier_semaphore()
-    for step in range(1, ranks):
-        pl.semaphore_signal(
-            barrier, inc=1, device_id={"kern": lax.rem(rank + step, ranks)}, device_id_type=MESH
-        )
+    for other in range(1, ranks):
+
+        @pl.when(other > rank)
+        def _():
+            pl.semaphore_signal(barrier, inc=1, device_id={"kern": other}, device_id_type=MESH)
+
     for other in (up, down):
         pl.semaphore_signal(barrier, inc=1, device_id={"tile": other}, device_id_type=MESH)
 
@@ -128,23 +135,26 @@
 
     get_hr.wait()
     get_hi.wait()
-    root = jnp.sqrt(jnp.full((KF, 2 * KF), weight[0], F32))
+    root = jnp.sqrt(jnp.full((KF, 2 * KF), weight[0, 0], F32))
     spec_all[rank] = (jnp.concatenate([hr[...], hi[...]], 1) * root).astype(BF16)
 
-    pl.semaphore_wait(barrier, ranks + 1)
-
-    spec_copies = []
-    for step in range(1, ranks):
-        copy = pltpu.make_async_remote_copy(
-            src_ref=spec_all.at[rank],
-            dst_ref=spec_all.at[rank],
-            send_sem=spec_send.at[step],
-            recv_sem=spec_recv.at[step],
-            device_id={"kern": lax.rem(rank + step, ranks)},
+    pl.semaphore_wait(barrier, rank + 2)
+
+    def spec_copy(source, other):
+        return pltpu.make_async_remote_copy(
+            src_ref=spec_all.at[source],
+            dst_ref=spec_all.at[source],
+            send_sem=spec_send.at[other],
+            recv_sem=spec_recv.at[source],
+            device_id={"kern": other},
             device_id_type=MESH,
         )
-        copy.start()
-        spec_copies.append(copy)
+
+    for other in range(ranks - 1):
+
+        @pl.when(other < rank)
+        def _():
+            spec_copy(rank, other).start()
 
     def to_neighbours(src, dst_up, dst_down, first):
         copies = []
@@ -213,37 +223,53 @@
         return jnp.where(low, both, other), jnp.where(low, other, both)
 
     get_rows.wait()
-    for copy in spec_copies:
-        copy.wait_recv()
-    for k in range(ranks):
-        real, imag = kernel_parts(k)
-        product = real * spec + imag * spec_turned
-        stacked[0:KF, k * LANES : (k + 1) * LANES] = product.astype(BF16)
-        stacked[KF:, k * LANES : (k + 1) * LANES] = (swap(product) * minus).astype(BF16)
-    for k in range(0, ranks, 2):
-        pair = dot(rows[...], stacked[:, k * LANES : (k + 2) * LANES]).astype(BF16)
-        lines[k * count : (k + 1) * count] = pair[:, :LANES]
-        lines[(k + 1) * count : (k + 2) * count] = pair[:, LANES:]
+    intensity[...] = jnp.zeros_like(intensity)
+    pair_rows = GROUP * count
+
+    def arrive(i, carry):
+        for k in range(GROUP):
+            other = i * GROUP + k
+
+            @pl.when(other != rank)
+            def _():
+                spec_copy(other, rank).wait_recv()
+
+            @pl.when(other > rank)
+            def _():
+                spec_copy(rank, other).start()
+
+            real, imag = kernel_parts(other)
+            product = real * spec + imag * spec_turned
+            stacked[0:KF, k * LANES : (k + 1) * LANES] = product.astype(BF16)
+            stacked[KF:, k * LANES : (k + 1) * LANES] = (swap(product) * minus).astype(BF16)
+        both = dot(rows[...], stacked[...]).astype(BF16)
+        line = jnp.concatenate([both[:, k * LANES : (k + 1) * LANES] for k in range(GROUP)], 0)
+        place = pl.ds(pl.multiple_of(i * pair_rows, 32), pair_rows)
+        for j in range(CHUNKS):
+            field = dot(line, to_cols[j])
+            total = intensity[:, j * LANES : (j + 1) * LANES]
+            for k in range(GROUP):
+                one = field[k * count : (k + 1) * count]
+                total = total + (one[:, :LANES] * one[:, :LANES] + one[:, LANES:] * one[:, LANES:])
+            intensity[:, j * LANES : (j + 1) * LANES] = total
+            fields[j, place] = field.astype(BF16)
+        return carry
+
+    lax.fori_loop(0, ranks // GROUP, arrive, 0)
     partial[...] = jnp.zeros_like(partial)
     get_target.wait()
-
-    size = GROUP * count
+    size = BATCH * count
 
     def chunk(j, carry):
-        total = jnp.zeros((count, LANES), F32)
-        for b in range(ranks // GROUP):
-            field = dot(lines[b * size : (b + 1) * size], to_cols[j])
-            for i in range(GROUP):
-                one = field[i * count : (i + 1) * count]
-                total = total + (one[:, :LANES] * one[:, :LANES] + one[:, LANES:] * one[:, LANES:])
-            fields[b * size : (b + 1) * size] = field.astype(BF16)
-        wanted = target[:, pl.ds(pl.multiple_of(j * LANES, LANES), LANES)].astype(F32)
+        place = pl.ds(pl.multiple_of(j * LANES, LANES), LANES)
+        total = intensity[:, place]
         resist = 1.0 / (1.0 + jnp.exp(-STEEPNESS * (total - THRESHOLD)))
+        wanted = target[:, place].astype(F32)
         slope = (2.0 * (resist - wanted) * STEEPNESS * resist * (1.0 - resist)).astype(BF16)
         slope = jnp.concatenate([slope, slope], 1)
-        slope = jnp.concatenate([slope] * GROUP, 0)
-        for b in range(ranks // GROUP):
-            weighted = fields[b * size : (b + 1) * size] * slope
+        slope = jnp.concatenate([slope] * BATCH, 0)
+        for b in range(ranks // BATCH):
+            weighted = fields[j, b * size : (b + 1) * size] * slope
             partial[b * size : (b + 1) * size] += dot(weighted, from_cols[j])
         return carry
 
@@ -267,24 +293,51 @@
             grad = grad + real * one + imag * (swap(one) * plus)
     part_all[rank] = (grad * (2.0 / (NE * KF))).astype(BF16)
 
-    part_copies = []
-    for step in range(1, ranks):
-        copy = pltpu.make_async_remote_copy(
-            src_ref=part_all.at[rank],
-            dst_ref=part_all.at[rank],
-            send_sem=part_send.at[step],
-            recv_sem=part_recv.at[step],
-            device_id={"kern": lax.rem(rank + step, ranks)},
+    def part_copy(source, hub):
+        return pltpu.make_async_remote_copy(
+            src_ref=part_all.at[source],
+            dst_ref=part_all.at[source],
+            send_sem=part_send.at[hub],
+            recv_sem=part_recv.at[source],
+            device_id={"kern": hub},
             device_id_type=MESH,
         )
-        copy.start()
-        part_copies.append(copy)
-    for copy in part_copies:
-        copy.wait_recv()
-    grad = jnp.zeros((KF, 2 * KF), F32)
-    for k in range(ranks):
-        grad = grad + part_all[k].astype(F32)
-    grad = grad.astype(BF16).astype(F32)
+
+    def sum_copy(other):
+        return pltpu.make_async_remote_copy(
+            src_ref=whole,
+            dst_ref=whole,
+            send_sem=sum_send.at[other],
+            recv_sem=sum_recv.at[0],
+            device_id={"kern": other},
+            device_id_type=MESH,
+        )
+
+    for hub in range(HUBS):
+
+        @pl.when(rank != hub)
+        def _():
+            part_copy(rank, hub).start()
+
+    @pl.when(rank < HUBS)
+    def _():
+        total = jnp.zeros((KF, 2 * KF), F32)
+        for source in range(ranks):
+
+            @pl.when(source != rank)
+            def _():
+                part_copy(source, 0).wait_recv()
+
+            total = total + part_all[source].astype(F32)
+        whole[...] = total.astype(BF16)
+        for step in range(1, ranks // HUBS):
+            sum_copy(rank + step * HUBS).start()
+
+    @pl.when(rank >= HUBS)
+    def _():
+        sum_copy(rank).wait_recv()
+
+    grad = whole[...].astype(F32)
     both = jnp.concatenate([grad, swap(grad) * minus], 0).astype(BF16)
     line = dot(rows[...], both)
     side = lax.broadcasted_iota(jnp.int32, (count, 2 * KF), 1) < KF
@@ -301,8 +354,24 @@
     out_ref[:, N - LANES : N] += jnp.where(
         jnp.logical_and(jnp.logical_not(side), tile < tiles - 1), margin_high[...], 0.0
     )
-    for copy in spec_copies + halo_copies + part_copies + margin_copies:
+    for copy in halo_copies + margin_copies:
         copy.wait_send()
+    for other in range(ranks):
+
+        @pl.when(other != rank)
+        def _():
+            spec_copy(rank, other).wait_send()
+
+    for hub in range(HUBS):
+
+        @pl.when(rank != hub)
+        def _():
+            part_copy(rank, hub).wait_send()
+
+    @pl.when(rank < HUBS)
+    def _():
+        for step in range(1, ranks // HUBS):
+            sum_copy(rank + step * HUBS).wait_send()
 
 
 def solution(mesh):
@@ -334,11 +403,12 @@
                 pltpu.VMEM((LANES, LANES), BF16),
                 pltpu.VMEM((LANES, LANES), BF16),
                 pltpu.VMEM((LANES, N), BF16),
-                pltpu.VMEM((LANES, ranks * LANES), BF16),
-                pltpu.VMEM((N, LANES), BF16),
+                pltpu.VMEM((LANES, GROUP * LANES), BF16),
+                pltpu.VMEM((count, N), F32),
+                pltpu.VMEM((KF, LANES), BF16),
                 pltpu.VMEM((CHUNKS, LANES, 2 * LANES), BF16),
                 pltpu.VMEM((CHUNKS, 2 * LANES, LANES), BF16),
-                pltpu.VMEM((N, 2 * LANES), BF16),
+                pltpu.VMEM((CHUNKS, N, 2 * LANES), BF16),
                 pltpu.VMEM((N, LANES), F32),
                 pltpu.VMEM((count, LANES), F32),
                 pltpu.VMEM((count, LANES), F32),
@@ -348,13 +418,15 @@
                 pltpu.SemaphoreType.DMA((ranks,)),
                 pltpu.SemaphoreType.DMA((ranks,)),
                 pltpu.SemaphoreType.DMA((ranks,)),
+                pltpu.SemaphoreType.DMA((ranks,)),
+                pltpu.SemaphoreType.DMA((1,)),
                 pltpu.SemaphoreType.DMA((4,)),
                 pltpu.SemaphoreType.DMA((4,)),
             ],
             compiler_params=pltpu.CompilerParams(collective_id=0, has_side_effects=True),
         )(
             orientation,
-            eigen_weights,
+            eigen_weights.reshape(1, 1),
             mask,
             target,
             kernel_real,

time: 65.6 us -> 123 us (1.88)
  the two profiles are of different devices: /device:TPU:17 before, /device:TPU:1 now
where the time goes in v2:
time: 123 us; the launch traced here: 121 us
  Pallas kernels  119 us (97%)
  local copies, waits for them, and re-layouts  1.64 us (1%)
    pallas_call x1, Pallas kernels, per_device(): pl.pallas_call(lambda *refs: body(ranks, *refs), out_shape=jax.ShapeDtype...  119 us

profile of v2, /device:TPU:1, one launch (start us, length us, event | category | flops | bytes accessed | tf_op | source)
XLA Modules:
  0.0 121.5 jit_solution(12450887195947154931)
XLA Ops:
  0.7 119.2 %shard_map.109 = f32[48,1152]{1,0:T(8,128)} custom-call(s32[1,2]{1,0:T(1,128)} %refs_0_.1, f32[1,1]{1,0:T(1,128)} %bitcast.1.refs_1_, bf16[1152,1152]{1,0:T(8,128)(2,1)} %refs_2_.1, s32[48,1152]{1,0:T(8,128)} %refs_3_.1, f32[1,64,64]{2,1,0:T(8,128)} %refs_4_.1, f32[1,64,64]{2,1,0:T(8,128)} %refs_5_.1, bf16[1152,128]{1,0:T(8,128)(2,1)} %constant.10.clone.refs_6_, ...), custom_call_target="tpu_custom_call" | custom-call | tf_op jit(solution)/shard_map/pallas_call | solution.py:386
  119.8 1.6 %copy.14 = f32[48,1152]{1,0:T(8,128)} copy(f32[48,1152]{1,0:T(8,128)} %shard_map.109) | data formatting | bytes 442368

commit v3 on v2

--- a/solution.py
+++ b/solution.py
@@ -18,6 +18,7 @@
 GROUP = 2
 BATCH = 4
 HUBS = 2
+LAST = 3
 
 STEEPNESS = 4.0
 THRESHOLD = 1.0
@@ -171,6 +172,18 @@
             copies.append(copy)
         return copies
 
+    pairs = ranks // GROUP
+    own = rank // GROUP
+    late = pairs - LAST
+    is_late = own >= late
+    ahead = jnp.where(is_late, pairs - own, late - own)
+
+    def turn(i):
+        past = i - ahead
+        nearest = jnp.where(past % 2 == 0, own - 1 - past // 2, past // 2)
+        early = jnp.where(past < own, own - 1 - past, late + past - own)
+        return jnp.where(past < 0, own + i, jnp.where(is_late, nearest, early))
+
     get_mid_t.wait()
     get_first.wait()
     get_last.wait()
@@ -227,8 +240,9 @@
     pair_rows = GROUP * count
 
     def arrive(i, carry):
+        at = turn(i)
         for k in range(GROUP):
-            other = i * GROUP + k
+            other = at * GROUP + k
 
             @pl.when(other != rank)
             def _():
@@ -289,7 +303,7 @@
         for i in range(2):
             one = wave[:, i * LANES : (i + 1) * LANES]
             one = one[:KF] + swap(one[KF:]) * plus
-            real, imag = kernel_parts(k + i)
+            real, imag = kernel_parts(turn(k // GROUP) * GROUP + i)
             grad = grad + real * one + imag * (swap(one) * plus)
     part_all[rank] = (grad * (2.0 / (NE * KF))).astype(BF16)
 

time: 123 us -> 72.3 us (0.59)
  the two profiles are of different devices: /device:TPU:1 before, /device:TPU:72 now
where the time goes in v3:
time: 72.3 us; the launch traced here: 72.1 us
  Pallas kernels  69.8 us (97%)
  local copies, waits for them, and re-layouts  1.64 us (2%)
    pallas_call x1, Pallas kernels, per_device(): pl.pallas_call(lambda *refs: body(ranks, *refs), out_shape=jax.ShapeDtype...  69.8 us
    unnamed x1, local copies, waits for them, and re-layouts  1.64 us

profile of v3, /device:TPU:72, one launch (start us, length us, event | category | flops | bytes accessed | tf_op | source)
XLA Modules:
  0.0 72.1 jit_solution(14019367121529410129)
XLA Ops:
  0.7 69.8 %shard_map.109 = f32[48,1152]{1,0:T(8,128)} custom-call(s32[1,2]{1,0:T(1,128)} %refs_0_.1, f32[1,1]{1,0:T(1,128)} %bitcast.1.refs_1_, bf16[1152,1152]{1,0:T(8,128)(2,1)} %refs_2_.1, s32[48,1152]{1,0:T(8,128)} %refs_3_.1, f32[1,64,64]{2,1,0:T(8,128)} %refs_4_.1, f32[1,64,64]{2,1,0:T(8,128)} %refs_5_.1, bf16[1152,128]{1,0:T(8,128)(2,1)} %constant.10.clone.refs_6_, ...), custom_call_target="tpu_custom_call" | custom-call | tf_op jit(solution)/shard_map/pallas_call | solution.py:400
  70.5 1.6 %copy.14 = f32[48,1152]{1,0:T(8,128)} copy(f32[48,1152]{1,0:T(8,128)} %shard_map.109) | data formatting | bytes 442368

commit v4 on v3

--- a/solution.py
+++ b/solution.py
@@ -12,13 +12,14 @@
 N = 1152
 HALO = 64
 KF = 64
+HALF = KF // 2
 NE = 1280
 LANES = 128
 CHUNKS = N // LANES
 GROUP = 2
 BATCH = 4
-HUBS = 2
 LAST = 3
+AHEAD = 3
 
 STEEPNESS = 4.0
 THRESHOLD = 1.0
@@ -70,13 +71,14 @@
     rows_t,
     spec_all,
     part_all,
+    share,
+    window,
     strip,
     halo_low,
     halo_high,
     columns,
     stacked,
     intensity,
-    whole,
     to_cols,
     from_cols,
     fields,
@@ -87,10 +89,11 @@
     local_sem,
     spec_send,
     spec_recv,
+    cross_send,
+    cross_recv,
     part_send,
     part_recv,
-    sum_send,
-    sum_recv,
+    here,
     tile_send,
     tile_recv,
 ):
@@ -134,17 +137,36 @@
     def swap(x):
         return pltpu.roll(x, KF, 1)
 
+    pl.semaphore_wait(barrier, rank + 2)
+
+    for other in range(ranks - 1):
+
+        @pl.when(other < rank)
+        def _():
+            pl.semaphore_signal(here.at[rank], inc=1, device_id={"kern": other}, device_id_type=MESH)
+
     get_hr.wait()
     get_hi.wait()
     root = jnp.sqrt(jnp.full((KF, 2 * KF), weight[0, 0], F32))
-    spec_all[rank] = (jnp.concatenate([hr[...], hi[...]], 1) * root).astype(BF16)
-
-    pl.semaphore_wait(barrier, rank + 2)
+    spectrum = (jnp.concatenate([hr[...], hi[...]], 1) * root).astype(BF16)
+    spec_all[rank, 0] = spectrum[:HALF]
+    spec_all[rank, 1] = spectrum[HALF:]
+    core = lax.rem(tile, 2)
+
+    def cross_copy(source):
+        return pltpu.make_async_remote_copy(
+            src_ref=spec_all.at[source, core],
+            dst_ref=spec_all.at[source, core],
+            send_sem=cross_send.at[source],
+            recv_sem=cross_recv.at[source],
+            device_id={"tile": tile + 1 - 2 * core},
+            device_id_type=MESH,
+        )
 
     def spec_copy(source, other):
         return pltpu.make_async_remote_copy(
-            src_ref=spec_all.at[source],
-            dst_ref=spec_all.at[source],
+            src_ref=spec_all.at[source, core],
+            dst_ref=spec_all.at[source, core],
             send_sem=spec_send.at[other],
             recv_sem=spec_recv.at[source],
             device_id={"kern": other},
@@ -174,15 +196,32 @@
 
     pairs = ranks // GROUP
     own = rank // GROUP
-    late = pairs - LAST
-    is_late = own >= late
-    ahead = jnp.where(is_late, pairs - own, late - own)
+    ahead = pairs - own
+    is_late = own >= pairs - LAST
 
     def turn(i):
         past = i - ahead
         nearest = jnp.where(past % 2 == 0, own - 1 - past // 2, past // 2)
-        early = jnp.where(past < own, own - 1 - past, late + past - own)
-        return jnp.where(past < 0, own + i, jnp.where(is_late, nearest, early))
+        early = jnp.where(is_late, nearest, own - 1 - past)
+        return jnp.where(past < 0, own + i, early)
+
+    def relay(at):
+        for k in range(GROUP):
+            other = at * GROUP + k
+
+            @pl.when(other != rank)
+            def _():
+                spec_copy(other, rank).wait_recv()
+                cross_copy(other).start()
+
+    def answer(at):
+        for k in range(GROUP):
+            other = at * GROUP + k
+
+            @pl.when(jnp.logical_and(other > rank, other < ranks))
+            def _():
+                pl.semaphore_wait(here.at[other], 1)
+                spec_copy(rank, other).start()
 
     get_mid_t.wait()
     get_first.wait()
@@ -231,7 +270,7 @@
     spec_turned = swap(spec) * minus
 
     def kernel_parts(k):
-        both = spec_all[k].astype(F32)
+        both = spec_all[k].reshape(KF, 2 * KF).astype(F32)
         other = swap(both)
         return jnp.where(low, both, other), jnp.where(low, other, both)
 
@@ -241,16 +280,18 @@
 
     def arrive(i, carry):
         at = turn(i)
+        answer(own + i + AHEAD)
+
+        @pl.when(i + 1 < pairs)
+        def _():
+            relay(turn(i + 1))
+
         for k in range(GROUP):
             other = at * GROUP + k
 
             @pl.when(other != rank)
             def _():
-                spec_copy(other, rank).wait_recv()
-
-            @pl.when(other > rank)
-            def _():
-                spec_copy(rank, other).start()
+                cross_copy(other).wait_recv()
 
             real, imag = kernel_parts(other)
             product = real * spec + imag * spec_turned
@@ -269,6 +310,9 @@
             fields[j, place] = field.astype(BF16)
         return carry
 
+    for i in range(AHEAD):
+        answer(own + i)
+    relay(own)
     lax.fori_loop(0, ranks // GROUP, arrive, 0)
     partial[...] = jnp.zeros_like(partial)
     get_target.wait()
@@ -305,53 +349,39 @@
             one = one[:KF] + swap(one[KF:]) * plus
             real, imag = kernel_parts(turn(k // GROUP) * GROUP + i)
             grad = grad + real * one + imag * (swap(one) * plus)
-    part_all[rank] = (grad * (2.0 / (NE * KF))).astype(BF16)
-
-    def part_copy(source, hub):
-        return pltpu.make_async_remote_copy(
-            src_ref=part_all.at[source],
-            dst_ref=part_all.at[source],
-            send_sem=part_send.at[hub],
-            recv_sem=part_recv.at[source],
-            device_id={"kern": hub},
+    def ring_copy(src, slot, turn_by, flip):
+        to = lax.rem(own + turn_by, pairs) * GROUP + (lax.rem(rank, GROUP) if not flip else 1 - lax.rem(rank, GROUP))
+        copy = pltpu.make_async_remote_copy(
+            src_ref=src,
+            dst_ref=part_all.at[slot],
+            send_sem=part_send.at[slot],
+            recv_sem=part_recv.at[slot],
+            device_id={"kern": to},
             device_id_type=MESH,
         )
-
-    def sum_copy(other):
-        return pltpu.make_async_remote_copy(
-            src_ref=whole,
-            dst_ref=whole,
-            send_sem=sum_send.at[other],
-            recv_sem=sum_recv.at[0],
-            device_id={"kern": other},
-            device_id_type=MESH,
-        )
-
-    for hub in range(HUBS):
-
-        @pl.when(rank != hub)
-        def _():
-            part_copy(rank, hub).start()
-
-    @pl.when(rank < HUBS)
-    def _():
-        total = jnp.zeros((KF, 2 * KF), F32)
-        for source in range(ranks):
-
-            @pl.when(source != rank)
-            def _():
-                part_copy(source, 0).wait_recv()
-
-            total = total + part_all[source].astype(F32)
-        whole[...] = total.astype(BF16)
-        for step in range(1, ranks // HUBS):
-            sum_copy(rank + step * HUBS).start()
-
-    @pl.when(rank >= HUBS)
-    def _():
-        sum_copy(rank).wait_recv()
-
-    grad = whole[...].astype(F32)
+        copy.start()
+        return copy
+
+    share[...] = (grad * (2.0 / (NE * KF))).astype(BF16)
+    near = [
+        ring_copy(share, slot, turn_by, flip)
+        for slot, (turn_by, flip) in enumerate(
+            ((pairs - 1, False), (pairs - 1, True), (1, False), (1, True), (0, True))
+        )
+    ]
+    total = share[...].astype(F32)
+    for slot, copy in enumerate(near):
+        copy.wait_recv()
+        total = total + part_all[slot].astype(F32)
+    window[...] = total.astype(BF16)
+    far = [
+        ring_copy(window, len(near) + slot, turn_by, False)
+        for slot, turn_by in enumerate((pairs // 2, pairs // 4, pairs - pairs // 4))
+    ]
+    for slot, copy in enumerate(far):
+        copy.wait_recv()
+        total = total + part_all[len(near) + slot].astype(F32)
+    grad = total.astype(BF16).astype(F32)
     both = jnp.concatenate([grad, swap(grad) * minus], 0).astype(BF16)
     line = dot(rows[...], both)
     side = lax.broadcasted_iota(jnp.int32, (count, 2 * KF), 1) < KF
@@ -368,24 +398,14 @@
     out_ref[:, N - LANES : N] += jnp.where(
         jnp.logical_and(jnp.logical_not(side), tile < tiles - 1), margin_high[...], 0.0
     )
-    for copy in halo_copies + margin_copies:
+    for copy in halo_copies + near + far + margin_copies:
         copy.wait_send()
     for other in range(ranks):
 
         @pl.when(other != rank)
         def _():
             spec_copy(rank, other).wait_send()
-
-    for hub in range(HUBS):
-
-        @pl.when(rank != hub)
-        def _():
-            part_copy(rank, hub).wait_send()
-
-    @pl.when(rank < HUBS)
-    def _():
-        for step in range(1, ranks // HUBS):
-            sum_copy(rank + step * HUBS).wait_send()
+            cross_copy(other).wait_send()
 
 
 def solution(mesh):
@@ -411,15 +431,16 @@
                 pltpu.VMEM((LANES, N), BF16),
                 pltpu.VMEM((count, LANES), BF16),
                 pltpu.VMEM((LANES, count), BF16),
-                pltpu.VMEM((ranks, KF, LANES), BF16),
-                pltpu.VMEM((ranks, KF, LANES), BF16),
+                pltpu.VMEM((ranks, 2, HALF, LANES), BF16),
+                pltpu.VMEM((8, KF, LANES), BF16),
+                pltpu.VMEM((KF, LANES), BF16),
+                pltpu.VMEM((KF, LANES), BF16),
                 pltpu.VMEM((LANES, LANES), BF16),
                 pltpu.VMEM((LANES, LANES), BF16),
                 pltpu.VMEM((LANES, LANES), BF16),
                 pltpu.VMEM((LANES, N), BF16),
                 pltpu.VMEM((LANES, GROUP * LANES), BF16),
                 pltpu.VMEM((count, N), F32),
-                pltpu.VMEM((KF, LANES), BF16),
                 pltpu.VMEM((CHUNKS, LANES, 2 * LANES), BF16),
                 pltpu.VMEM((CHUNKS, 2 * LANES, LANES), BF16),
                 pltpu.VMEM((CHUNKS, N, 2 * LANES), BF16),
@@ -433,7 +454,8 @@
                 pltpu.SemaphoreType.DMA((ranks,)),
                 pltpu.SemaphoreType.DMA((ranks,)),
                 pltpu.SemaphoreType.DMA((ranks,)),
-                pltpu.SemaphoreType.DMA((1,)),
+                pltpu.SemaphoreType.DMA((ranks,)),
+                pltpu.SemaphoreType.REGULAR((ranks,)),
                 pltpu.SemaphoreType.DMA((4,)),
                 pltpu.SemaphoreType.DMA((4,)),
             ],

time: 72.3 us -> 59.8 us (0.83)
  the two profiles are of different devices: /device:TPU:72 before, /device:TPU:1 now
where the time goes in v4:
time: 59.8 us; the launch traced here: 59.2 us
  Pallas kernels  56.9 us (95%)
  local copies, waits for them, and re-layouts  1.64 us (3%)
  between operations  0.66 us (1%)
    pallas_call x1, Pallas kernels, per_device(): pl.pallas_call(lambda *refs: body(ranks, *refs), out_shape=jax.ShapeDtype...  56.9 us
    unnamed x1, local copies, waits for them, and re-layouts  1.64 us

profile of v4, /device:TPU:1, one launch (start us, length us, event | category | flops | bytes accessed | tf_op | source)
XLA Modules:
  0.0 59.2 jit_solution(17349840732883984220)
XLA Ops:
  0.7 56.9 %shard_map.109 = f32[48,1152]{1,0:T(8,128)} custom-call(s32[1,2]{1,0:T(1,128)} %refs_0_.1, f32[1,1]{1,0:T(1,128)} %bitcast.1.refs_1_, bf16[1152,1152]{1,0:T(8,128)(2,1)} %refs_2_.1, s32[48,1152]{1,0:T(8,128)} %refs_3_.1, f32[1,64,64]{2,1,0:T(8,128)} %refs_4_.1, f32[1,64,64]{2,1,0:T(8,128)} %refs_5_.1, bf16[1152,128]{1,0:T(8,128)(2,1)} %constant.10.clone.refs_6_, ...), custom_call_target="tpu_custom_call" | custom-call | tf_op jit(solution)/shard_map/pallas_call | solution.py:420
  57.6 1.6 %copy.14 = f32[48,1152]{1,0:T(8,128)} copy(f32[48,1152]{1,0:T(8,128)} %shard_map.109) | data formatting | bytes 442368

commit v5 on v4

--- a/solution.py
+++ b/solution.py
@@ -18,8 +18,8 @@
 CHUNKS = N // LANES
 GROUP = 2
 BATCH = 4
-LAST = 3
 AHEAD = 3
+HELPED = 4
 
 STEEPNESS = 4.0
 THRESHOLD = 1.0
@@ -63,6 +63,7 @@
     out_ref,
     mask,
     target,
+    wanted,
     hr,
     hi,
     mid,
@@ -83,6 +84,7 @@
     from_cols,
     fields,
     partial,
+    gradient,
     margin,
     margin_low,
     margin_high,
@@ -94,6 +96,7 @@
     part_send,
     part_recv,
     here,
+    target_sem,
     tile_send,
     tile_recv,
 ):
@@ -126,9 +129,14 @@
     get_last = load(mask_hbm.at[:, N - LANES : N], mask.at[:, N - LANES : N], 4)
     get_inner = load(mask_hbm.at[:, LANES : N - LANES], mask.at[:, LANES : N - LANES], 5)
     get_mid = load(mid_hbm, mid, 6)
-    get_rows = load(mid_hbm.at[pl.ds(pl.multiple_of(rank * count, 16), count)], rows, 7)
-    get_rows_t = load(rows_t_hbm.at[rank], rows_t, 8)
-    get_target = load(target_hbm, target, 9)
+    get_target = load(target_hbm, target, 7)
+    workers = ranks - HELPED
+    whose = (rank, lax.rem(rank + workers, ranks))
+    get_rows = [
+        load(mid_hbm.at[pl.ds(pl.multiple_of(owner * count, 16), count)], rows.at[s], 8 + s)
+        for s, owner in enumerate(whose)
+    ]
+    get_rows_t = [load(rows_t_hbm.at[owner], rows_t.at[s], 10 + s) for s, owner in enumerate(whose)]
 
     low = lax.broadcasted_iota(jnp.int32, (KF, 2 * KF), 1) < KF
     plus = jnp.where(low, 1.0, -1.0)
@@ -141,7 +149,7 @@
 
     for other in range(ranks - 1):
 
-        @pl.when(other < rank)
+        @pl.when(jnp.logical_and(other < rank, jnp.logical_or(rank < workers, other >= workers)))
         def _():
             pl.semaphore_signal(here.at[rank], inc=1, device_id={"kern": other}, device_id_type=MESH)
 
@@ -173,7 +181,7 @@
             device_id_type=MESH,
         )
 
-    for other in range(ranks - 1):
+    for other in range(workers):
 
         @pl.when(other < rank)
         def _():
@@ -197,13 +205,10 @@
     pairs = ranks // GROUP
     own = rank // GROUP
     ahead = pairs - own
-    is_late = own >= pairs - LAST
 
     def turn(i):
         past = i - ahead
-        nearest = jnp.where(past % 2 == 0, own - 1 - past // 2, past // 2)
-        early = jnp.where(is_late, nearest, own - 1 - past)
-        return jnp.where(past < 0, own + i, early)
+        return jnp.where(past < 0, own + i, own - 1 - past)
 
     def relay(at):
         for k in range(GROUP):
@@ -218,7 +223,7 @@
         for k in range(GROUP):
             other = at * GROUP + k
 
-            @pl.when(jnp.logical_and(other > rank, other < ranks))
+            @pl.when(jnp.logical_and(other > rank, other < workers))
             def _():
                 pl.semaphore_wait(here.at[other], 1)
                 spec_copy(rank, other).start()
@@ -274,9 +279,38 @@
         other = swap(both)
         return jnp.where(low, both, other), jnp.where(low, other, both)
 
-    get_rows.wait()
-    intensity[...] = jnp.zeros_like(intensity)
+    for copy in [get_target] + get_rows + get_rows_t:
+        copy.wait()
+    wanted[0] = target[...].astype(F32).astype(BF16)
+    target_copy = pltpu.make_async_remote_copy(
+        src_ref=wanted.at[0],
+        dst_ref=wanted.at[1],
+        send_sem=target_sem.at[0],
+        recv_sem=target_sem.at[1],
+        device_id={"kern": lax.rem(rank + HELPED, ranks)},
+        device_id_type=MESH,
+    )
+
+    @pl.when(rank >= workers)
+    def _():
+        for other in range(workers):
+            spec_copy(rank, other).wait_send()
+        target_copy.start()
+
     pair_rows = GROUP * count
+
+    def forward(i, s):
+        both = dot(rows[s], stacked[...]).astype(BF16)
+        line = jnp.concatenate([both[:, k * LANES : (k + 1) * LANES] for k in range(GROUP)], 0)
+        place = pl.ds(pl.multiple_of(i * pair_rows, 32), pair_rows)
+        for j in range(CHUNKS):
+            field = dot(line, to_cols[j])
+            total = intensity[s, :, j * LANES : (j + 1) * LANES]
+            for k in range(GROUP):
+                one = field[k * count : (k + 1) * count]
+                total = total + (one[:, :LANES] * one[:, :LANES] + one[:, LANES:] * one[:, LANES:])
+            intensity[s, :, j * LANES : (j + 1) * LANES] = total
+            fields[s, j, place] = field.astype(BF16)
 
     def arrive(i, carry):
         at = turn(i)
@@ -297,58 +331,60 @@
             product = real * spec + imag * spec_turned
             stacked[0:KF, k * LANES : (k + 1) * LANES] = product.astype(BF16)
             stacked[KF:, k * LANES : (k + 1) * LANES] = (swap(product) * minus).astype(BF16)
-        both = dot(rows[...], stacked[...]).astype(BF16)
-        line = jnp.concatenate([both[:, k * LANES : (k + 1) * LANES] for k in range(GROUP)], 0)
-        place = pl.ds(pl.multiple_of(i * pair_rows, 32), pair_rows)
-        for j in range(CHUNKS):
-            field = dot(line, to_cols[j])
-            total = intensity[:, j * LANES : (j + 1) * LANES]
-            for k in range(GROUP):
-                one = field[k * count : (k + 1) * count]
-                total = total + (one[:, :LANES] * one[:, :LANES] + one[:, LANES:] * one[:, LANES:])
-            intensity[:, j * LANES : (j + 1) * LANES] = total
-            fields[j, place] = field.astype(BF16)
+        forward(i, 0)
+
+        @pl.when(rank < HELPED)
+        def _():
+            forward(i, 1)
+
         return carry
 
-    for i in range(AHEAD):
-        answer(own + i)
-    relay(own)
-    lax.fori_loop(0, ranks // GROUP, arrive, 0)
-    partial[...] = jnp.zeros_like(partial)
-    get_target.wait()
     size = BATCH * count
 
-    def chunk(j, carry):
-        place = pl.ds(pl.multiple_of(j * LANES, LANES), LANES)
-        total = intensity[:, place]
-        resist = 1.0 / (1.0 + jnp.exp(-STEEPNESS * (total - THRESHOLD)))
-        wanted = target[:, place].astype(F32)
-        slope = (2.0 * (resist - wanted) * STEEPNESS * resist * (1.0 - resist)).astype(BF16)
-        slope = jnp.concatenate([slope, slope], 1)
-        slope = jnp.concatenate([slope] * BATCH, 0)
-        for b in range(ranks // BATCH):
-            weighted = fields[j, b * size : (b + 1) * size] * slope
-            partial[b * size : (b + 1) * size] += dot(weighted, from_cols[j])
-        return carry
-
-    lax.fori_loop(0, CHUNKS, chunk, 0)
-
-    get_rows_t.wait()
-    grad = jnp.zeros((KF, 2 * KF), F32)
-    for k in range(0, ranks, 2):
-        pair = jnp.concatenate(
-            [
-                partial[k * count : (k + 1) * count].astype(BF16),
-                partial[(k + 1) * count : (k + 2) * count].astype(BF16),
-            ],
-            1,
-        )
-        wave = dot(rows_t[...], pair)
-        for i in range(2):
-            one = wave[:, i * LANES : (i + 1) * LANES]
-            one = one[:KF] + swap(one[KF:]) * plus
-            real, imag = kernel_parts(turn(k // GROUP) * GROUP + i)
-            grad = grad + real * one + imag * (swap(one) * plus)
+    def adjoint(s):
+        def chunk(j, carry):
+            place = pl.ds(pl.multiple_of(j * LANES, LANES), LANES)
+            total = intensity[s, :, place]
+            resist = 1.0 / (1.0 + jnp.exp(-STEEPNESS * (total - THRESHOLD)))
+            pattern = wanted[s, :, place].astype(F32)
+            slope = (2.0 * (resist - pattern) * STEEPNESS * resist * (1.0 - resist)).astype(BF16)
+            slope = jnp.concatenate([slope, slope], 1)
+            slope = jnp.concatenate([slope] * BATCH, 0)
+            for b in range(ranks // BATCH):
+                weighted = fields[s, j, b * size : (b + 1) * size] * slope
+                partial[b * size : (b + 1) * size] += dot(weighted, from_cols[j])
+            return carry
+
+        partial[...] = jnp.zeros_like(partial)
+        lax.fori_loop(0, CHUNKS, chunk, 0)
+
+        grad = jnp.zeros((KF, 2 * KF), F32)
+        for k in range(0, ranks, 2):
+            pair = [partial[(k + i) * count : (k + i + 1) * count].astype(BF16) for i in range(2)]
+            wave = dot(rows_t[s], jnp.concatenate(pair, 1))
+            for i in range(2):
+                one = wave[:, i * LANES : (i + 1) * LANES]
+                one = one[:KF] + swap(one[KF:]) * plus
+                real, imag = kernel_parts(turn(k // GROUP) * GROUP + i)
+                grad = grad + real * one + imag * (swap(one) * plus)
+        gradient[...] += grad * (2.0 / (NE * KF))
+
+    gradient[...] = jnp.zeros_like(gradient)
+
+    @pl.when(rank < workers)
+    def _():
+        intensity[...] = jnp.zeros_like(intensity)
+        for i in range(AHEAD):
+            answer(own + i)
+        relay(own)
+        lax.fori_loop(0, pairs, arrive, 0)
+        adjoint(0)
+
+    @pl.when(rank < HELPED)
+    def _():
+        target_copy.wait_recv()
+        adjoint(1)
+
     def ring_copy(src, slot, turn_by, flip):
         to = lax.rem(own + turn_by, pairs) * GROUP + (lax.rem(rank, GROUP) if not flip else 1 - lax.rem(rank, GROUP))
         copy = pltpu.make_async_remote_copy(
@@ -362,7 +398,13 @@
         copy.start()
         return copy
 
-    share[...] = (grad * (2.0 / (NE * KF))).astype(BF16)
+    for other in range(workers + 1, ranks):
+
+        @pl.when(jnp.logical_and(rank >= workers, other > rank))
+        def _():
+            pl.semaphore_wait(here.at[other], 1)
+
+    share[...] = gradient[...].astype(BF16)
     near = [
         ring_copy(share, slot, turn_by, flip)
         for slot, (turn_by, flip) in enumerate(
@@ -383,7 +425,7 @@
         total = total + part_all[len(near) + slot].astype(F32)
     grad = total.astype(BF16).astype(F32)
     both = jnp.concatenate([grad, swap(grad) * minus], 0).astype(BF16)
-    line = dot(rows[...], both)
+    line = dot(rows[0], both)
     side = lax.broadcasted_iota(jnp.int32, (count, 2 * KF), 1) < KF
     line = jnp.where(side, line, -line).astype(BF16)
     first_lanes = lax.broadcasted_iota(jnp.int32, (LANES, LANES), 1) < HALO
@@ -400,11 +442,21 @@
     )
     for copy in halo_copies + near + far + margin_copies:
         copy.wait_send()
+
+    @pl.when(rank >= workers)
+    def _():
+        target_copy.wait_send()
+
+    for other in range(workers):
+
+        @pl.when(jnp.logical_and(other != rank, rank < workers))
+        def _():
+            spec_copy(rank, other).wait_send()
+
     for other in range(ranks):
 
-        @pl.when(other != rank)
-        def _():
-            spec_copy(rank, other).wait_send()
+        @pl.when(jnp.logical_and(other != rank, rank < workers))
+        def _():
             cross_copy(other).wait_send()
 
 
@@ -425,12 +477,13 @@
             scratch_shapes=[
                 pltpu.VMEM((N, N), BF16),
                 pltpu.VMEM((count, N), jnp.int32),
+                pltpu.VMEM((2, count, N), BF16),
                 pltpu.VMEM((KF, KF), F32),
                 pltpu.VMEM((KF, KF), F32),
                 pltpu.VMEM((N, LANES), BF16),
                 pltpu.VMEM((LANES, N), BF16),
-                pltpu.VMEM((count, LANES), BF16),
-                pltpu.VMEM((LANES, count), BF16),
+                pltpu.VMEM((2, count, LANES), BF16),
+                pltpu.VMEM((2, LANES, count), BF16),
                 pltpu.VMEM((ranks, 2, HALF, LANES), BF16),
                 pltpu.VMEM((8, KF, LANES), BF16),
                 pltpu.VMEM((KF, LANES), BF16),
@@ -440,15 +493,16 @@
                 pltpu.VMEM((LANES, LANES), BF16),
                 pltpu.VMEM((LANES, N), BF16),
                 pltpu.VMEM((LANES, GROUP * LANES), BF16),
-                pltpu.VMEM((count, N), F32),
+                pltpu.VMEM((2, count, N), F32),
                 pltpu.VMEM((CHUNKS, LANES, 2 * LANES), BF16),
                 pltpu.VMEM((CHUNKS, 2 * LANES, LANES), BF16),
-                pltpu.VMEM((CHUNKS, N, 2 * LANES), BF16),
+                pltpu.VMEM((2, CHUNKS, N, 2 * LANES), BF16),
                 pltpu.VMEM((N, LANES), F32),
+                pltpu.VMEM((KF, LANES), F32),
                 pltpu.VMEM((count, LANES), F32),
                 pltpu.VMEM((count, LANES), F32),
                 pltpu.VMEM((count, LANES), F32),
-                pltpu.SemaphoreType.DMA((10,)),
+                pltpu.SemaphoreType.DMA((12,)),
                 pltpu.SemaphoreType.DMA((ranks,)),
                 pltpu.SemaphoreType.DMA((ranks,)),
                 pltpu.SemaphoreType.DMA((ranks,)),
@@ -456,6 +510,7 @@
                 pltpu.SemaphoreType.DMA((ranks,)),
                 pltpu.SemaphoreType.DMA((ranks,)),
                 pltpu.SemaphoreType.REGULAR((ranks,)),
+                pltpu.SemaphoreType.DMA((2,)),
                 pltpu.SemaphoreType.DMA((4,)),
                 pltpu.SemaphoreType.DMA((4,)),
             ],

time: 59.8 us -> 58.1 us (0.972)
  Pallas kernels: 56.9 us -> 55.6 us
    pallas_call x1, Pallas kernels: 56.9 us -> 55.6 us  [per_device(): pl.pallas_call(lambda *refs: body(ranks, *refs), out_shape=jax.ShapeDtype...]
where the time goes in v5:
time: 58.1 us; the launch traced here: 57.9 us
  Pallas kernels  55.6 us (96%)
  local copies, waits for them, and re-layouts  1.64 us (3%)
  between operations  0.66 us (1%)
    pallas_call x1, Pallas kernels, per_device(): pl.pallas_call(lambda *refs: body(ranks, *refs), out_shape=jax.ShapeDtype...  55.6 us
    unnamed x1, local copies, waits for them, and re-layouts  1.64 us

profile of v5, /device:TPU:1, one launch (start us, length us, event | category | flops | bytes accessed | tf_op | source)
XLA Modules:
  0.0 57.9 jit_solution(5753853473743010751)
XLA Ops:
  0.7 55.6 %shard_map.109 = f32[48,1152]{1,0:T(8,128)} custom-call(s32[1,2]{1,0:T(1,128)} %refs_0_.1, f32[1,1]{1,0:T(1,128)} %bitcast.1.refs_1_, bf16[1152,1152]{1,0:T(8,128)(2,1)} %refs_2_.1, s32[48,1152]{1,0:T(8,128)} %refs_3_.1, f32[1,64,64]{2,1,0:T(8,128)} %refs_4_.1, f32[1,64,64]{2,1,0:T(8,128)} %refs_5_.1, bf16[1152,128]{1,0:T(8,128)(2,1)} %constant.10.clone.refs_6_, ...), custom_call_target="tpu_custom_call" | custom-call | tf_op jit(solution)/shard_map/pallas_call | solution.py:472
  56.2 1.6 %copy.14 = f32[48,1152]{1,0:T(8,128)} copy(f32[48,1152]{1,0:T(8,128)} %shard_map.109) | data formatting | bytes 442368

commit v6 on v5

--- a/solution.py
+++ b/solution.py
@@ -181,7 +181,7 @@
             device_id_type=MESH,
         )
 
-    for other in range(workers):
+    for other in sorted(range(workers), key=lambda o: abs(o - ranks // 2 + 1)):
 
         @pl.when(other < rank)
         def _():

time: 58.1 us -> 56.8 us (0.978)
  Pallas kernels: 55.6 us -> 54.2 us
    pallas_call x1, Pallas kernels: 55.6 us -> 54.2 us  [per_device(): pl.pallas_call(lambda *refs: body(ranks, *refs), out_shape=jax.ShapeDtype...]
where the time goes in v6:
time: 56.8 us; the launch traced here: 56.5 us
  Pallas kernels  54.2 us (95%)
  local copies, waits for them, and re-layouts  1.64 us (3%)
  between operations  0.66 us (1%)
    pallas_call x1, Pallas kernels, per_device(): pl.pallas_call(lambda *refs: body(ranks, *refs), out_shape=jax.ShapeDtype...  54.2 us
    unnamed x1, local copies, waits for them, and re-layouts  1.64 us

profile of v6, /device:TPU:1, one launch (start us, length us, event | category | flops | bytes accessed | tf_op | source)
XLA Modules:
  0.0 56.5 jit_solution(2405446652841934067)
XLA Ops:
  0.7 54.2 %shard_map.109 = f32[48,1152]{1,0:T(8,128)} custom-call(s32[1,2]{1,0:T(1,128)} %refs_0_.1, f32[1,1]{1,0:T(1,128)} %bitcast.1.refs_1_, bf16[1152,1152]{1,0:T(8,128)(2,1)} %refs_2_.1, s32[48,1152]{1,0:T(8,128)} %refs_3_.1, f32[1,64,64]{2,1,0:T(8,128)} %refs_4_.1, f32[1,64,64]{2,1,0:T(8,128)} %refs_5_.1, bf16[1152,128]{1,0:T(8,128)(2,1)} %constant.10.clone.refs_6_, ...), custom_call_target="tpu_custom_call" | custom-call | tf_op jit(solution)/shard_map/pallas_call | solution.py:472
  54.9 1.6 %copy.14 = f32[48,1152]{1,0:T(8,128)} copy(f32[48,1152]{1,0:T(8,128)} %shard_map.109) | data formatting | bytes 442368
